TPU v7x, 32 devices: a whole 2x2x4 slice. The times are simulated.
32 devices in a mesh: groups: 2 (over y), frame: 4 (over z), panel: 2 (over x), sub: 2 (over core).
Axes of the slice: x: 2, y: 2, z: 4, core: 2. Of those that a mesh axis runs over, the one named last changes fastest.
Arguments:
- frames: bfloat16 [2048, 65536], P(('groups', 'frame'), ('panel', 'sub')), parts along dimension 0, may hold values from -16 to 16
- slices: float32 [32, 65536], P(('groups', 'frame'), ('panel', 'sub')), parts along dimension 0, may hold values from -8 to 8
- log_prior: float32 [4096], replicated, may hold values from -2 to 2
- orient: int32 [32], P('groups'), parts along dimension 0, may hold values from 0 to 4095
Outputs:
- new_slices: float32 [32, 65536], P(('groups', 'frame'), ('panel', 'sub')), parts along dimension 0
There are 2 independent parts, one for each index of `groups`. A program takes and returns all parts, laid end to end along the dimension named above; an argument that names none is the same for every part. Nothing has to cross between parts.
All inputs are finite; a program needn't handle non-finite values.
Results may differ from a plain program's by a relative error of at most 0.022.
The roundings to bfloat16 on the way count: a program that leaves them out, or rounds other values in their place, can miss the bound.
Values may be sent and summed in bfloat16 or wider, within the bound.
A program may use at most 64 MiB of HBM per device.

v0:
```python
import math
import jax
import jax.numpy as jnp
from jax import lax
from jax.sharding import PartitionSpec as P

PIX = 65536
ITERS = 2


def fetch_slices(owned_b):
    return lax.all_gather(owned_b, "frame", axis=0, tiled=True)


def owner_update(weights, frames, counts, owned_b, offset):
    owned = owned_b.shape[0]
    mine = lax.psum_scatter(
        jnp.einsum("fm,fp->mp", weights, frames, preferred_element_type=jnp.float32).astype(
            jnp.bfloat16
        ),
        "frame",
        scatter_dimension=0,
        tiled=True,
    ).astype(jnp.float32)
    my_counts = lax.dynamic_slice_in_dim(counts, offset, owned, 0)
    return (mine + owned_b.astype(jnp.float32)) / (my_counts + 1.0)[:, None]


def local(frames, slices, log_prior, orient):
    owned = slices.shape[0]
    temper = 3.0 / math.sqrt(PIX)
    matches = orient[:, None] == jnp.arange(log_prior.shape[0], dtype=jnp.int32)[None, :]
    prior = jnp.sum(jnp.where(matches, log_prior[None, :], 0.0), axis=1)
    offset = lax.axis_index("frame") * owned
    current = slices
    owned_b = slices.astype(jnp.bfloat16)
    for step in range(ITERS):
        if step == 0:
            gathered = fetch_slices(owned_b)
        else:
            gathered = fetch_slices(owned_b)
        wide = gathered.astype(jnp.float32)
        norms = jnp.sum(wide * wide, axis=1)
        raw = (
            jnp.einsum("fp,mp->fm", frames, gathered, preferred_element_type=jnp.float32)
            - 0.5 * norms[None, :]
        )
        summed = lax.psum(raw, ("panel", "sub"))
        weights = jax.nn.softmax(temper * summed + prior[None, :], axis=1).astype(jnp.bfloat16)
        counts = lax.psum(jnp.sum(weights.astype(jnp.float32), axis=0), "frame")
        if step + 1 < ITERS:
            current = owner_update(weights, frames, counts, owned_b, offset)
            owned_b = current.astype(jnp.bfloat16)
        else:
            current = owner_update(weights, frames, counts, owned_b, offset)
    return current


def solution(mesh):
    in_specs = (
        P(("groups", "frame"), ("panel", "sub")),
        P(("groups", "frame"), ("panel", "sub")),
        P(),
        P("groups"),
    )
    out_specs = P(("groups", "frame"), ("panel", "sub"))
    return jax.shard_map(local, mesh=mesh, in_specs=in_specs, out_specs=out_specs, check_vma=False)
```

profile of v0, /device:TPU:0, one launch (start us, length us, event | category | flops | bytes accessed | tf_op | source)
XLA Modules:
  0.0 173.9 jit_solution(4613914813418080331)
XLA Ops:
  6.5 0.0 copy-start.2
  6.5 0.0 copy-start.1
  6.5 0.0 all-reduce.5.cloned.1.call-start
  6.5 1.0 convert_bitcast_fusion
  7.6 17.4 %all-gather = bf16[4,4,16384]{2,1,0:T(4,128)(2,1)S(1)} all-gather(bf16[1,4,16384]{2,1,0:T(4,128)(2,1)S(1)} %convert_bitcast_fusion), channel_id=1, replica_groups=mesh['groups'=2,'frame'=4,'panel'=2,'sub'=2] {'frame'}, dimensions={0}, use_global_device_ids=true | all-gather | bytes 655360 | tf_op jit(solution)/shard_map/all_gather | solution.py:12
  24.9 0.1 reshape.18
  25.1 0.2 multiply_reduce_fusion.1
  25.3 0.0 copy-start.3
  25.3 0.0 copy-start
  25.3 5.7 %convolution_subtract_fusion.1 = f32[256,16]{0,1:T(8,128)S(1)} fusion(bf16[256,16384]{1,0:T(8,128)(2,1)} %param.4, bf16[16,16384]{1,0:T(8,128)(2,1)S(1)} %reshape.18, f32[16]{0:T(128)S(1)} %broadcast_multiply_fusion.1), kind=kOutput, calls=%fused_computation.4 | convolution fusion | flops 134221824 | bytes 8929344 | tf_op jit(solution)/shard_map/fp,mp->fm/dot_general | solution.py:45
  31.0 10.1 %psum.28 = f32[256,16]{0,1:T(8,128)S(1)} all-reduce(f32[256,16]{0,1:T(8,128)S(1)} %convolution_subtract_fusion.1), channel_id=1, replica_groups=mesh['groups'=2,'frame'=4,'panel'=2,'sub'=2] {'panel','sub'}, use_global_device_ids=true, to_apply=%region_1.2 | all-reduce | flops 4096 | bytes 32768 | tf_op jit(solution)/shard_map/psum | solution.py:48
  41.1 0.0 copy-done.2
  41.1 0.0 copy-done.1
  41.1 0.2 select_reduce_fusion
  41.4 0.1 fusion.2
  41.5 0.1 fusion.4
  41.6 0.2 convert_reduce_fusion.1
  41.7 5.4 %convolution_convert_fusion.1 = bf16[16,16384]{1,0:T(8,128)(2,1)} fusion(bf16[256,16]{0,1:T(8,128)(2,1)S(1)} %get-tuple-element.8, bf16[256,16384]{1,0:T(8,128)(2,1)} %param.4), kind=kOutput, calls=%fused_computation.1 | convolution fusion | flops 134479872 | bytes 8921088 | tf_op jit(solution)/shard_map/fm,fp->mp/dot_general | solution.py:18
  47.2 0.0 all-reduce.5.cloned.1.call-update
  47.2 0.0 all-reduce.7.cloned.1.call-start
  47.2 0.0 copy-done.3
  47.3 0.6 dynamic-slice
  48.5 12.6 %psum.29 = f32[16]{0:T(128)S(1)} all-reduce(f32[16]{0:T(128)S(1)} %get-tuple-element.7), channel_id=1, replica_groups=mesh['groups'=2,'frame'=4,'panel'=2,'sub'=2] {'frame'}, use_global_device_ids=true, to_apply=%region_7.8 | all-reduce | flops 16 | bytes 128 | tf_op jit(solution)/shard_map/psum | solution.py:50
  61.0 0.1 dynamic-slice_add_fusion.1
  61.1 26.4 %all-reduce.5.cloned.1.call-done = bf16[16,16384]{1,0:T(8,128)(2,1)} async-done(((bf16[16,16384]{1,0:T(8,128)(2,1)}), bf16[16,16384]{1,0:T(8,128)(2,1)}) %all-reduce.5.cloned.1.call-update) | async-done | bytes 524304
  87.6 0.0 copy-done
  87.6 1.1 fusion.1
  88.6 16.2 %all-gather.1 = bf16[4,4,16384]{2,1,0:T(4,128)(2,1)S(1)} all-gather(bf16[1,4,16384]{2,1,0:T(4,128)(2,1)S(1)} %bitcast.14), channel_id=1, replica_groups=mesh['groups'=2,'frame'=4,'panel'=2,'sub'=2] {'frame'}, dimensions={0}, use_global_device_ids=true | all-gather | bytes 655360 | tf_op jit(solution)/shard_map/all_gather | solution.py:12
  104.8 0.1 reshape.20
  104.9 0.2 multiply_reduce_fusion
  105.2 5.6 %fusion = f32[256,16]{0,1:T(8,128)S(1)} fusion(bf16[16,16384]{1,0:T(8,128)(2,1)S(1)} %reshape.20, bf16[256,16384]{1,0:T(8,128)(2,1)} %param.4, f32[16]{0:T(128)S(1)} %broadcast_multiply_fusion), kind=kOutput, calls=%fused_computation.3 | convolution fusion | flops 134221824 | bytes 8929344 | tf_op jit(solution)/shard_map/fp,mp->fm/dot_general | solution.py:45
  110.8 10.1 %psum.30 = f32[256,16]{0,1:T(8,128)S(1)} all-reduce(f32[256,16]{0,1:T(8,128)S(1)} %fusion), channel_id=1, replica_groups=mesh['groups'=2,'frame'=4,'panel'=2,'sub'=2] {'panel','sub'}, use_global_device_ids=true, to_apply=%region_9.10 | all-reduce | flops 4096 | bytes 32768 | tf_op jit(solution)/shard_map/psum | solution.py:48
  120.9 0.1 fusion.3
  121.0 0.1 fusion.5
  121.1 0.2 convert_reduce_fusion
  121.3 5.4 %convolution_convert_fusion = bf16[16,16384]{1,0:T(8,128)(2,1)} fusion(bf16[256,16]{0,1:T(8,128)(2,1)S(1)} %get-tuple-element.6, bf16[256,16384]{1,0:T(8,128)(2,1)} %param.4), kind=kOutput, calls=%fused_computation | convolution fusion | flops 134479872 | bytes 8921088 | tf_op jit(solution)/shard_map/fm,fp->mp/dot_general | solution.py:18
  126.7 0.0 all-reduce.7.cloned.1.call-update
  126.7 10.8 %psum.31 = f32[16]{0:T(128)S(1)} all-reduce(f32[16]{0:T(128)S(1)} %get-tuple-element.5), channel_id=1, replica_groups=mesh['groups'=2,'frame'=4,'panel'=2,'sub'=2] {'frame'}, use_global_device_ids=true, to_apply=%region_14.15 | all-reduce | flops 16 | bytes 128 | tf_op jit(solution)/shard_map/psum | solution.py:50
  137.5 0.1 dynamic-slice_add_fusion
  137.6 27.7 %all-reduce.7.cloned.1.call-done = bf16[16,16384]{1,0:T(8,128)(2,1)} async-done(((bf16[16,16384]{1,0:T(8,128)(2,1)}), bf16[16,16384]{1,0:T(8,128)(2,1)}) %all-reduce.7.cloned.1.call-update) | async-done | bytes 524304
  165.3 1.8 %add_divide_fusion = f32[4,16384]{1,0:T(4,128)} fusion(bf16[4,16384]{1,0:T(4,128)(2,1)S(1)} %fusion.1, bf16[16,16384]{1,0:T(8,128)(2,1)} %all-reduce.7.cloned.1.call-done, u32[]{:T(128)S(6)} %multiply.1, f32[4]{0:T(128)S(1)} %dynamic-slice_add_fusion), kind=kLoop, calls=%fused_computation.7 | loop fusion | flops 262144 | bytes 524308 | tf_op jit(solution)/shard_map/div | solution.py:26
  (2 shorter events, 0.0 us)
Async XLA Ops:
  6.5 34.6 %copy-start.2 = (s32[16]{0:T(128)S(1)}, s32[16]{0:T(128)}, u32[]{:S(2)}) copy-start(s32[16]{0:T(128)} %param.7) | copy-start | bytes 196
  6.5 34.6 %copy-start.1 = (f32[4096]{0:T(1024)S(1)}, f32[4096]{0:T(1024)}, u32[]{:S(2)}) copy-start(f32[4096]{0:T(1024)} %param.6) | copy-start | bytes 49156
  6.5 81.0 %all-reduce.5.cloned.1.call-start = ((), (), s32[]{:S(2)}) async-start(), calls=%async_computation | async-start | bytes 1048576
  25.3 21.9 %copy-start.3 = (u32[32]{0:T(128)S(1)}, u32[32]{0:T(128)}, u32[]{:S(2)}) copy-start(u32[32]{0:T(128)} %constant.25) | copy-start | bytes 388
  25.3 62.2 %copy-start = (f32[4,16384]{1,0:T(4,128)S(1)}, f32[4,16384]{1,0:T(4,128)}, u32[]{:S(2)}) copy-start(f32[4,16384]{1,0:T(4,128)} %param.5) | copy-start | bytes 786436
  47.2 118.2 %all-reduce.7.cloned.1.call-start = ((), (), s32[]{:S(2)}) async-start(), calls=%async_computation.1 | async-start | bytes 1048576
Sparse Core Ops, SparseCore 0:
  47.3 40.1 all-reduce.4
  126.9 38.4 all-reduce.6
where the time goes:
time: 174 us
  blocking collectives  77.1 us (44%)
  waiting for transfers between devices  54.2 us (31%)
  matrix products  22.2 us (13%)
  between operations  14.1 us (8%)
  other arithmetic  5.48 us (3%)
    unnamed x4, waiting for transfers between devices  54.2 us
    all_gather x2, blocking collectives, fetch_slices(): return lax.all_gather(owned_b, 'frame', axis=0, tiled=True)  33.5 us
    psum x2, blocking collectives, local(): counts = lax.psum(jnp.sum(weights.astype(jnp.float32), axis=0), 'frame')  23.3 us
    psum x2, blocking collectives, local(): summed = lax.psum(raw, ('panel', 'sub'))  20.2 us
    dot_general x2, matrix products, local(): jnp.einsum('fp,mp->fm', frames, gathered, preferred_element_type=jnp.floa...  11.3 us
    dot_general x2, matrix products, owner_update(): jnp.einsum('fm,fp->mp', weights, frames, preferred_element_type=jnp.float32)  10.8 us
  transfers between devices with their start and end apart: 2, of which 2 were waited for; matrix products, arithmetic and copies ran while one was open for 0% of the time, Pallas kernels for 0%

commit v1 on v0

--- a/solution.py
+++ b/solution.py
@@ -45,7 +45,7 @@
             jnp.einsum("fp,mp->fm", frames, gathered, preferred_element_type=jnp.float32)
             - 0.5 * norms[None, :]
         )
-        summed = lax.psum(raw, ("panel", "sub"))
+        summed = jnp.sum(lax.all_gather(raw, ("panel", "sub")), axis=0)
         weights = jax.nn.softmax(temper * summed + prior[None, :], axis=1).astype(jnp.bfloat16)
         counts = lax.psum(jnp.sum(weights.astype(jnp.float32), axis=0), "frame")
         if step + 1 < ITERS:

time: 174 us -> 165 us (0.948)
  blocking collectives: 77.1 us -> 67.4 us
    psum x2 -> x0, blocking collectives: 20.2 us -> none  [local(): summed = lax.psum(raw, ('panel', 'sub'))]
    all_gather x0 -> x2, blocking collectives: none -> 10.5 us  [local(): summed = jnp.sum(lax.all_gather(raw, ('panel', 'sub')), axis=0)]
where the time goes in v1:
time: 165 us; the launch traced here: 164 us
  blocking collectives  67.4 us (41%)
  waiting for transfers between devices  53.9 us (33%)
  matrix products  22.2 us (13%)
  between operations  14.2 us (9%)
  other arithmetic  5.55 us (3%)
    unnamed x4, waiting for transfers between devices  53.9 us
    all_gather x2, blocking collectives, fetch_slices(): return lax.all_gather(owned_b, 'frame', axis=0, tiled=True)  33.5 us
    psum x2, blocking collectives, local(): counts = lax.psum(jnp.sum(weights.astype(jnp.float32), axis=0), 'frame')  23.3 us
    dot_general x2, matrix products, local(): jnp.einsum('fp,mp->fm', frames, gathered, preferred_element_type=jnp.floa...  11.3 us
    dot_general x2, matrix products, owner_update(): jnp.einsum('fm,fp->mp', weights, frames, preferred_element_type=jnp.float32)  10.8 us
    all_gather x2, blocking collectives, local(): summed = jnp.sum(lax.all_gather(raw, ('panel', 'sub')), axis=0)  10.5 us
  transfers between devices with their start and end apart: 2, of which 2 were waited for; matrix products, arithmetic and copies ran while one was open for 0% of the time, Pallas kernels for 0%

profile of v1, /device:TPU:0, one launch (start us, length us, event | category | flops | bytes accessed | tf_op | source)
XLA Modules:
  0.0 164.1 jit_solution(12453963066606732000)
XLA Ops:
  6.5 0.0 copy-start.2
  6.5 0.0 copy-start.1
  6.5 0.0 all-reduce.5.cloned.1.call-start
  6.5 1.0 convert_bitcast_fusion
  7.6 17.4 %all-gather.2 = bf16[4,4,16384]{2,1,0:T(4,128)(2,1)S(1)} all-gather(bf16[1,4,16384]{2,1,0:T(4,128)(2,1)S(1)} %convert_bitcast_fusion), channel_id=1, replica_groups=mesh['groups'=2,'frame'=4,'panel'=2,'sub'=2] {'frame'}, dimensions={0}, use_global_device_ids=true | all-gather | bytes 655360 | tf_op jit(solution)/shard_map/all_gather | solution.py:12
  24.9 0.1 reshape.20
  25.1 0.2 multiply_reduce_fusion.1
  25.3 0.0 copy-start.3
  25.3 0.0 copy-start
  25.3 5.7 %convolution_subtract_fusion.1 = f32[256,16]{0,1:T(8,128)S(1)} fusion(bf16[256,16384]{1,0:T(8,128)(2,1)} %param.4, bf16[16,16384]{1,0:T(8,128)(2,1)S(1)} %reshape.20, f32[16]{0:T(128)S(1)} %broadcast_multiply_fusion.1), kind=kOutput, calls=%fused_computation.4 | convolution fusion | flops 134221824 | bytes 8929344 | tf_op jit(solution)/shard_map/fp,mp->fm/dot_general | solution.py:45
  31.0 5.2 %all-gather = f32[1024,16]{0,1:T(8,128)S(1)} all-gather(f32[256,16]{0,1:T(8,128)S(1)} %convolution_subtract_fusion.1), channel_id=2, replica_groups=mesh['groups'=2,'frame'=4,'panel'=2,'sub'=2] {'panel','sub'}, dimensions={0}, use_global_device_ids=true | all-gather | bytes 81920 | tf_op jit(solution)/shard_map/all_gather | solution.py:48
  36.3 0.0 copy-done.2
  36.3 0.0 copy-done.1
  36.3 0.2 select_reduce_fusion
  36.6 0.1 fusion.2
  36.7 0.1 fusion.4
  36.8 0.2 convert_reduce_fusion.1
  37.0 5.4 %convolution_convert_fusion.1 = bf16[16,16384]{1,0:T(8,128)(2,1)} fusion(bf16[256,16]{0,1:T(8,128)(2,1)S(1)} %get-tuple-element.8, bf16[256,16384]{1,0:T(8,128)(2,1)} %param.4), kind=kOutput, calls=%fused_computation.1 | convolution fusion | flops 134479872 | bytes 8921088 | tf_op jit(solution)/shard_map/fm,fp->mp/dot_general | solution.py:18
  42.4 0.0 all-reduce.5.cloned.1.call-update
  42.4 0.0 all-reduce.7.cloned.1.call-start
  42.5 0.0 copy-done.3
  42.5 0.6 dynamic-slice
  43.7 12.6 %psum.14 = f32[16]{0:T(128)S(1)} all-reduce(f32[16]{0:T(128)S(1)} %get-tuple-element.7), channel_id=1, replica_groups=mesh['groups'=2,'frame'=4,'panel'=2,'sub'=2] {'frame'}, use_global_device_ids=true, to_apply=%region_7.8 | all-reduce | flops 16 | bytes 128 | tf_op jit(solution)/shard_map/psum | solution.py:50
  56.3 0.1 dynamic-slice_add_fusion.1
  56.3 26.4 %all-reduce.5.cloned.1.call-done = bf16[16,16384]{1,0:T(8,128)(2,1)} async-done(((bf16[16,16384]{1,0:T(8,128)(2,1)}), bf16[16,16384]{1,0:T(8,128)(2,1)}) %all-reduce.5.cloned.1.call-update) | async-done | bytes 524304
  82.7 0.0 copy-done
  82.7 1.1 fusion.1
  83.8 16.2 %all-gather.3 = bf16[4,4,16384]{2,1,0:T(4,128)(2,1)S(1)} all-gather(bf16[1,4,16384]{2,1,0:T(4,128)(2,1)S(1)} %bitcast.18), channel_id=1, replica_groups=mesh['groups'=2,'frame'=4,'panel'=2,'sub'=2] {'frame'}, dimensions={0}, use_global_device_ids=true | all-gather | bytes 655360 | tf_op jit(solution)/shard_map/all_gather | solution.py:12
  99.9 0.1 reshape.22
  100.1 0.2 multiply_reduce_fusion
  100.3 5.6 %fusion = f32[256,16]{0,1:T(8,128)S(1)} fusion(bf16[16,16384]{1,0:T(8,128)(2,1)S(1)} %reshape.22, bf16[256,16384]{1,0:T(8,128)(2,1)} %param.4, f32[16]{0:T(128)S(1)} %broadcast_multiply_fusion), kind=kOutput, calls=%fused_computation.3 | convolution fusion | flops 134221824 | bytes 8929344 | tf_op jit(solution)/shard_map/fp,mp->fm/dot_general | solution.py:45
  106.0 5.2 %all-gather.1 = f32[1024,16]{0,1:T(8,128)S(1)} all-gather(f32[256,16]{0,1:T(8,128)S(1)} %fusion), channel_id=3, replica_groups=mesh['groups'=2,'frame'=4,'panel'=2,'sub'=2] {'panel','sub'}, dimensions={0}, use_global_device_ids=true | all-gather | bytes 81920 | tf_op jit(solution)/shard_map/all_gather | solution.py:48
  111.3 0.1 fusion.3
  111.4 0.1 fusion.5
  111.5 0.2 convert_reduce_fusion
  111.7 5.4 %convolution_convert_fusion = bf16[16,16384]{1,0:T(8,128)(2,1)} fusion(bf16[256,16]{0,1:T(8,128)(2,1)S(1)} %get-tuple-element.6, bf16[256,16384]{1,0:T(8,128)(2,1)} %param.4), kind=kOutput, calls=%fused_computation | convolution fusion | flops 134479872 | bytes 8921088 | tf_op jit(solution)/shard_map/fm,fp->mp/dot_general | solution.py:18
  117.1 0.0 all-reduce.7.cloned.1.call-update
  117.1 10.8 %psum.15 = f32[16]{0:T(128)S(1)} all-reduce(f32[16]{0:T(128)S(1)} %get-tuple-element.5), channel_id=1, replica_groups=mesh['groups'=2,'frame'=4,'panel'=2,'sub'=2] {'frame'}, use_global_device_ids=true, to_apply=%region_14.15 | all-reduce | flops 16 | bytes 128 | tf_op jit(solution)/shard_map/psum | solution.py:50
  127.9 0.1 dynamic-slice_add_fusion
  128.0 27.6 %all-reduce.7.cloned.1.call-done = bf16[16,16384]{1,0:T(8,128)(2,1)} async-done(((bf16[16,16384]{1,0:T(8,128)(2,1)}), bf16[16,16384]{1,0:T(8,128)(2,1)}) %all-reduce.7.cloned.1.call-update) | async-done | bytes 524304
  155.5 1.8 %add_divide_fusion = f32[4,16384]{1,0:T(4,128)} fusion(bf16[4,16384]{1,0:T(4,128)(2,1)S(1)} %fusion.1, bf16[16,16384]{1,0:T(8,128)(2,1)} %all-reduce.7.cloned.1.call-done, u32[]{:T(128)S(6)} %multiply.1, f32[4]{0:T(128)S(1)} %dynamic-slice_add_fusion), kind=kLoop, calls=%fused_computation.7 | loop fusion | flops 262144 | bytes 524308 | tf_op jit(solution)/shard_map/div | solution.py:26
  (6 shorter events, 0.2 us)
Async XLA Ops:
  6.5 29.8 %copy-start.2 = (s32[16]{0:T(128)S(1)}, s32[16]{0:T(128)}, u32[]{:S(2)}) copy-start(s32[16]{0:T(128)} %param.7) | copy-start | bytes 196
  6.5 29.8 %copy-start.1 = (f32[4096]{0:T(1024)S(1)}, f32[4096]{0:T(1024)}, u32[]{:S(2)}) copy-start(f32[4096]{0:T(1024)} %param.6) | copy-start | bytes 49156
  6.5 76.2 %all-reduce.5.cloned.1.call-start = ((), (), s32[]{:S(2)}) async-start(), calls=%async_computation | async-start | bytes 1048576
  25.3 17.2 %copy-start.3 = (u32[32]{0:T(128)S(1)}, u32[32]{0:T(128)}, u32[]{:S(2)}) copy-start(u32[32]{0:T(128)} %constant.25) | copy-start | bytes 388
  25.3 57.4 %copy-start = (f32[4,16384]{1,0:T(4,128)S(1)}, f32[4,16384]{1,0:T(4,128)}, u32[]{:S(2)}) copy-start(f32[4,16384]{1,0:T(4,128)} %param.5) | copy-start | bytes 786436
  42.4 113.1 %all-reduce.7.cloned.1.call-start = ((), (), s32[]{:S(2)}) async-start(), calls=%async_computation.1 | async-start | bytes 1048576
Sparse Core Ops, SparseCore 0:
  42.5 40.1 all-reduce.4
  117.2 38.2 all-reduce.6
